TPU v7x, 256 devices: a whole 4x4x8 slice. The times are simulated.
256 devices in a mesh: shard: 64 (over y, z, core), tensor: 4 (over x).
Axes of the slice: x: 4, y: 4, z: 8, core: 2. Of those that a mesh axis runs over, the one named last changes fastest.
Arguments:
- gradient: bfloat16 [64, 1024, 1024], P(None, 'shard', 'tensor'), may hold values from -64 to 64, as said below
- momentum: float32 [64, 1024, 1024], P(None, 'shard', 'tensor'), may hold values from -64 to 64, as said below
Outputs:
- momentum_out: float32 [64, 1024, 1024], P(None, 'shard', 'tensor')
- update: float32 [64, 1024, 1024], P(None, 'shard', 'tensor')
Inputs may be any that keep to these rules, and one draw needn't show every extreme that they name: `gradient`: finite real values. `momentum`: finite real values.
All inputs are finite; a program needn't handle non-finite values.
Results may differ from a plain program's by a relative error of at most 0.0003.
Values sent between devices are 32-bit elements; how exact they have to be, the bound alone decides.
No kernel may reach another device: no remote copies, remote signals or barrier semaphores. Data moves between devices by JAX's collectives and lax.ppermute only.
A program may use at most 64 MiB of HBM per device.

v0:
```python
import math
import jax
import jax.numpy as jnp
from jax import lax
from jax.sharding import PartitionSpec as P

D = 1024
BLOCK = 1024
ITERS = 3
first_coef = 3.4445
second_coef = -4.775
third_coef = 2.0315
decay_rate = 0.95


def product(left, right):
    return jnp.einsum(
        "ij,jl->il",
        left,
        right,
        precision=lax.Precision.HIGHEST,
        preferred_element_type=jnp.float32,
    )


def against(left, right):
    return jnp.einsum(
        "ij,lj->il",
        left,
        right,
        precision=lax.Precision.HIGHEST,
        preferred_element_type=jnp.float32,
    )


def per_device(gradient, momentum):
    widened = gradient.astype(jnp.float32)
    momentum_out = decay_rate * momentum + widened
    direction = widened + decay_rate * momentum_out
    by_owner = lax.all_to_all(direction, "shard", split_axis=0, concat_axis=0, tiled=True)
    row_pieces = lax.all_to_all(by_owner, "tensor", split_axis=1, concat_axis=2, tiled=True)
    piece_count = row_pieces.shape[0]
    piece_rows = row_pieces.shape[1]
    width = row_pieces.shape[2]
    iterate = row_pieces.reshape(piece_count * piece_rows, width)
    norm_total = lax.psum(jnp.sum(iterate * iterate), "tensor")
    iterate = iterate / (jnp.sqrt(norm_total) + 1e-07)
    for sweep_index in range(ITERS):
        full_rows = lax.all_gather(iterate, "tensor", axis=0, tiled=True)
        gram_rows = against(iterate, full_rows)
        full_gram = lax.all_gather(gram_rows, "tensor", axis=0, tiled=True)
        square_rows = product(gram_rows, full_gram)
        polynomial = second_coef * gram_rows + third_coef * square_rows
        iterate = first_coef * iterate + product(polynomial, full_rows)
    result = (0.2 * math.sqrt(max(BLOCK, D)) * iterate).reshape(piece_count, piece_rows, width)
    update = lax.all_to_all(
        lax.all_to_all(result, "shard", split_axis=0, concat_axis=0, tiled=True),
        "tensor",
        split_axis=2,
        concat_axis=1,
        tiled=True,
    )
    return (momentum_out, update)


def solution(mesh):
    placed = (P(None, "shard", "tensor"), P(None, "shard", "tensor"))
    return jax.shard_map(
        per_device,
        mesh=mesh,
        in_specs=placed,
        out_specs=(P(None, "shard", "tensor"), P(None, "shard", "tensor")),
        check_vma=False,
    )
```

profile of v0, /device:TPU:1, one launch (start us, length us, event | category | flops | bytes accessed | tf_op | source)
XLA Modules:
  0.0 516.5 jit_solution(14466420875342971486)
XLA Ops:
  7.2 0.0 all-gather.7.cloned.1.call-start
  7.2 2.6 convert_add_fusion
  9.8 41.5 %all_to_all.37 = f32[64,16,256]{2,1,0:T(8,128)S(1)} all-to-all(f32[64,16,256]{2,1,0:T(8,128)S(1)} %get-tuple-element.4), channel_id=1, replica_groups=mesh['shard'=64,'tensor'=4] {'shard'}, dimensions={0} | all-to-all | bytes 2097152 | tf_op jit(solution)/shard_map/all_to_all | solution.py:40
  51.2 0.6 copy.12
  51.8 18.7 %all_to_all.38 = f32[64,16,256]{2,0,1:T(8,128)S(1)} all-to-all(f32[64,16,256]{2,0,1:T(8,128)S(1)} %copy.12), channel_id=1, replica_groups=mesh['shard'=64,'tensor'=4] {'tensor'}, dimensions={1} | all-to-all | bytes 2097152 | tf_op jit(solution)/shard_map/all_to_all | solution.py:41
  70.5 0.9 multiply_reduce_fusion
  71.4 7.6 %psum.7 = f32[]{:T(128)} all-reduce(f32[]{:T(128)} %multiply_reduce_fusion), channel_id=1, replica_groups=mesh['shard'=64,'tensor'=4] {'tensor'}, use_global_device_ids=true, to_apply=%region_1.0 | all-reduce | flops 1 | bytes 8 | tf_op jit(solution)/shard_map/psum | solution.py:46
  79.6 0.1 broadcast_divide_fusion
  79.7 0.7 copy.13
  80.4 1.2 copy.16
  81.6 0.0 all-gather.7.cloned.1.call-update
  81.6 0.0 all-gather.9.cloned.1.call-start
  81.6 47.9 %all-gather.7.cloned.1.call-done = f32[1024,1024]{1,0:T(8,128)} async-done(((f32[256,1024]{1,0:T(8,128)}), f32[1024,1024]{1,0:T(8,128)}) %all-gather.7.cloned.1.call-update) | async-done | bytes 4194320 | tf_op jit(solution)/shard_map/all_gather | solution.py:49
  129.6 7.3 %fusion.4 = f32[256,1024]{1,0:T(8,128)} fusion(f32[256,1024]{1,0:T(8,128)} %bitcast.29, f32[1024,1024]{1,0:T(8,128)} %all-gather.7.cloned.1.call-done), kind=kOutput, calls=%fused_computation.14 | convolution fusion | flops 3221225472 | bytes 6291456 | tf_op jit(solution)/shard_map/ij,lj->il/dot_general | solution.py:27
  136.8 0.0 copy-start.5
  136.8 0.0 all-gather.9.cloned.1.call-update
  136.9 0.3 all-gather.11.cloned.1.call-start
  137.2 50.9 %all-gather.9.cloned.1.call-done = f32[1024,1024]{1,0:T(8,128)} async-done(((f32[256,1024]{1,0:T(8,128)}), f32[1024,1024]{1,0:T(8,128)}) %all-gather.9.cloned.1.call-update) | async-done | bytes 4194320 | tf_op jit(solution)/shard_map/all_gather | solution.py:51
  188.1 0.0 copy-start
  188.1 6.7 %fusion.3 = f32[256,1024]{1,0:T(8,128)S(1)} fusion(f32[256,1024]{1,0:T(8,128)} %fusion.4, f32[1024,1024]{1,0:T(8,128)} %all-gather.9.cloned.1.call-done), kind=kOutput, calls=%fused_computation.9 | convolution fusion | flops 3222011904 | bytes 6291456 | tf_op jit(solution)/shard_map/ij,jl->il/dot_general | solution.py:17
  194.8 0.0 copy-done.5
  194.8 0.0 copy-done
  194.8 4.7 convolution_add_fusion.2
  199.5 0.0 all-gather.11.cloned.1.call-update
  199.6 0.0 all-gather.13.cloned.1.call-start
  199.6 51.2 %all-gather.11.cloned.1.call-done = f32[1024,1024]{1,0:T(8,128)} async-done(((f32[256,1024]{1,0:T(8,128)}), f32[1024,1024]{1,0:T(8,128)}) %all-gather.11.cloned.1.call-update) | async-done | bytes 4194320 | tf_op jit(solution)/shard_map/all_gather | solution.py:49
  250.8 7.3 %fusion.5 = f32[256,1024]{1,0:T(8,128)} fusion(f32[256,1024]{1,0:T(8,128)} %convolution_add_fusion.2, f32[1024,1024]{1,0:T(8,128)} %all-gather.11.cloned.1.call-done), kind=kOutput, calls=%fused_computation.15 | convolution fusion | flops 3221225472 | bytes 6291456 | tf_op jit(solution)/shard_map/ij,lj->il/dot_general | solution.py:27
  258.1 0.0 copy-start.3
  258.1 0.0 all-gather.13.cloned.1.call-update
  258.1 0.6 all-gather.15.cloned.1.call-start
  258.7 50.7 %all-gather.13.cloned.1.call-done = f32[1024,1024]{1,0:T(8,128)} async-done(((f32[256,1024]{1,0:T(8,128)}), f32[1024,1024]{1,0:T(8,128)}) %all-gather.13.cloned.1.call-update) | async-done | bytes 4194320 | tf_op jit(solution)/shard_map/all_gather | solution.py:51
  309.4 0.0 copy-start.1
  309.4 6.7 %fusion.2 = f32[256,1024]{1,0:T(8,128)S(1)} fusion(f32[256,1024]{1,0:T(8,128)} %fusion.5, f32[1024,1024]{1,0:T(8,128)} %all-gather.13.cloned.1.call-done), kind=kOutput, calls=%fused_computation.6 | convolution fusion | flops 3222011904 | bytes 6291456 | tf_op jit(solution)/shard_map/ij,jl->il/dot_general | solution.py:17
  316.1 0.0 copy-done.3
  316.1 0.0 copy-done.1
  316.1 4.7 convolution_add_fusion.1
  320.8 0.0 all-gather.15.cloned.1.call-update
  320.8 0.2 all-gather.17.cloned.1.call-start
  321.0 51.0 %all-gather.15.cloned.1.call-done = f32[1024,1024]{1,0:T(8,128)} async-done(((f32[256,1024]{1,0:T(8,128)}), f32[1024,1024]{1,0:T(8,128)}) %all-gather.15.cloned.1.call-update) | async-done | bytes 4194320 | tf_op jit(solution)/shard_map/all_gather | solution.py:49
  372.1 7.3 %fusion.6 = f32[256,1024]{1,0:T(8,128)} fusion(f32[256,1024]{1,0:T(8,128)} %convolution_add_fusion.1, f32[1024,1024]{1,0:T(8,128)} %all-gather.15.cloned.1.call-done), kind=kOutput, calls=%fused_computation.16 | convolution fusion | flops 3221225472 | bytes 6291456 | tf_op jit(solution)/shard_map/ij,lj->il/dot_general | solution.py:27
  379.3 0.0 copy-start.4
  379.3 0.0 all-gather.17.cloned.1.call-update
  379.4 51.3 %all-gather.17.cloned.1.call-done = f32[1024,1024]{1,0:T(8,128)} async-done(((f32[256,1024]{1,0:T(8,128)}), f32[1024,1024]{1,0:T(8,128)}) %all-gather.17.cloned.1.call-update) | async-done | bytes 4194320 | tf_op jit(solution)/shard_map/all_gather | solution.py:51
  430.6 0.0 copy-start.2
  430.6 6.7 %fusion.1 = f32[256,1024]{1,0:T(8,128)S(1)} fusion(f32[256,1024]{1,0:T(8,128)} %fusion.6, f32[1024,1024]{1,0:T(8,128)} %all-gather.17.cloned.1.call-done), kind=kOutput, calls=%fused_computation.3 | convolution fusion | flops 3222011904 | bytes 6291456 | tf_op jit(solution)/shard_map/ij,jl->il/dot_general | solution.py:17
  437.3 0.0 copy-done.4
  437.3 0.0 copy-done.2
  437.3 3.8 fusion
  441.1 0.3 reshape.14
  441.4 39.4 %all_to_all.39 = f32[64,4,1024]{2,1,0:T(4,128)S(1)} all-to-all(f32[64,4,1024]{2,1,0:T(4,128)S(1)} %reshape.14), channel_id=1, replica_groups=mesh['shard'=64,'tensor'=4] {'shard'}, dimensions={0} | all-to-all | bytes 2097152 | tf_op jit(solution)/shard_map/all_to_all | solution.py:57
  480.8 0.9 copy.14
  481.7 2.0 reshape.15
  483.8 17.7 %all_to_all.40 = f32[4,1,65536]{2,1,0:T(1,128)S(1)} all-to-all(f32[4,1,65536]{2,1,0:T(1,128)S(1)} %reshape.15), channel_id=1, replica_groups=mesh['shard'=64,'tensor'=4] {'tensor'}, dimensions={0} | all-to-all | bytes 2097152 | tf_op jit(solution)/shard_map/all_to_all | solution.py:56
  501.4 0.5 broadcast.34
  501.9 3.7 reduce.3
  505.6 1.4 reshape.16
  507.1 1.0 copy.15
  508.1 1.3 all_to_all.32
Async XLA Ops:
  7.2 122.4 %all-gather.7.cloned.1.call-start = ((), (), s32[]{:S(2)}) async-start(), calls=%async_computation.4 | async-start | bytes 5242880 | tf_op jit(solution)/shard_map/all_gather | solution.py:49
  81.6 106.5 %all-gather.9.cloned.1.call-start = ((), (), s32[]{:S(2)}) async-start(), calls=%async_computation.5 | async-start | bytes 5242880 | tf_op jit(solution)/shard_map/all_gather | solution.py:51
  136.8 58.0 %copy-start.5 = (f32[32,8,4,256]{3,1,2,0:T(8,128)S(1)}, f32[32,8,4,256]{3,1,2,0:T(8,128)}, u32[]{:S(2)}) copy-start(f32[32,8,4,256]{3,1,2,0:T(8,128)} %copy.16) | copy-start | bytes 3145732
  136.9 114.0 %all-gather.11.cloned.1.call-start = ((), (), s32[]{:S(2)}) async-start(), calls=%async_computation.6 | async-start | bytes 5242880 | tf_op jit(solution)/shard_map/all_gather | solution.py:49
  188.1 6.7 %copy-start = (f32[1024,1024]{1,0:T(8,128)S(1)}, f32[1024,1024]{1,0:T(8,128)}, u32[]{:S(2)}) copy-start(f32[1024,1024]{1,0:T(8,128)} %all-gather.7.cloned.1.call-done) | copy-start | bytes 12582916
  199.6 109.8 %all-gather.13.cloned.1.call-start = ((), (), s32[]{:S(2)}) async-start(), calls=%async_computation.7 | async-start | bytes 5242880 | tf_op jit(solution)/shard_map/all_gather | solution.py:51
  258.1 58.0 %copy-start.3 = (f32[256,1024]{1,0:T(8,128)S(1)}, f32[256,1024]{1,0:T(8,128)}, u32[]{:S(2)}) copy-start(f32[256,1024]{1,0:T(8,128)} %convolution_add_fusion.2) | copy-start | bytes 3145732
  258.1 114.0 %all-gather.15.cloned.1.call-start = ((), (), s32[]{:S(2)}) async-start(), calls=%async_computation.8 | async-start | bytes 5242880 | tf_op jit(solution)/shard_map/all_gather | solution.py:49
  309.4 6.7 %copy-start.1 = (f32[1024,1024]{1,0:T(8,128)S(1)}, f32[1024,1024]{1,0:T(8,128)}, u32[]{:S(2)}) copy-start(f32[1024,1024]{1,0:T(8,128)} %all-gather.11.cloned.1.call-done) | copy-start | bytes 12582916
  320.8 109.8 %all-gather.17.cloned.1.call-start = ((), (), s32[]{:S(2)}) async-start(), calls=%async_computation.9 | async-start | bytes 5242880 | tf_op jit(solution)/shard_map/all_gather | solution.py:51
  379.3 58.0 %copy-start.4 = (f32[256,1024]{1,0:T(8,128)S(1)}, f32[256,1024]{1,0:T(8,128)}, u32[]{:S(2)}) copy-start(f32[256,1024]{1,0:T(8,128)} %convolution_add_fusion.1) | copy-start | bytes 3145732
  430.6 6.7 %copy-start.2 = (f32[1024,1024]{1,0:T(8,128)S(1)}, f32[1024,1024]{1,0:T(8,128)}, u32[]{:S(2)}) copy-start(f32[1024,1024]{1,0:T(8,128)} %all-gather.15.cloned.1.call-done) | copy-start | bytes 12582916
Sparse Core Ops, SparseCore 0:
  81.7 47.8 all-gather.6
  137.0 51.0 all-gather.8
  199.7 51.0 all-gather.10
  258.2 51.0 all-gather.12
  320.9 51.0 all-gather.14
  379.5 51.0 all-gather.16
where the time goes:
time: 522 us; the launch traced here: 517 us
  waiting for transfers between devices  303 us (58%)
  blocking collectives  125 us (24%)
  matrix products  55 us (11%)
  between operations  15.2 us (3%)
  local copies, waits for them, and re-layouts  10 us (2%)
  other arithmetic  7.21 us (1%)
    all_gather x3, waiting for transfers between devices, per_device(): full_gram = lax.all_gather(gram_rows, 'tensor', axis=0, tiled=True)  153 us
    all_gather x3, waiting for transfers between devices, per_device(): full_rows = lax.all_gather(iterate, 'tensor', axis=0, tiled=True)  150 us
    all_to_all x1, blocking collectives, per_device(): lax.all_to_all(direction, 'shard', split_axis=0, concat_axis=0, tiled=True)  41.5 us
    all_to_all x1, blocking collectives, per_device(): lax.all_to_all(result, 'shard', split_axis=0, concat_axis=0, tiled=True)  39.4 us
    dot_general x6, matrix products, product(): jnp.einsum('ij,jl->il', left, right, precision=lax.Precision.HIGHEST, pre...  33.2 us
    dot_general x3, matrix products, against(): jnp.einsum('ij,lj->il', left, right, precision=lax.Precision.HIGHEST, pre...  21.8 us
    all_to_all x1, blocking collectives, per_device(): lax.all_to_all(by_owner, 'tensor', split_axis=1, concat_axis=2, tiled=True)  18.7 us
    all_to_all x1, blocking collectives, per_device(): lax.all_to_all(lax.all_to_all(result, 'shard', split_axis=0, concat_axis=...  17.7 us
  transfers between devices with their start and end apart: 6, of which 6 were waited for; matrix products, arithmetic and copies ran while one was open for 0% of the time, Pallas kernels for 0%

commit v1 on v0

--- a/solution.py
+++ b/solution.py
@@ -48,7 +48,9 @@
     for sweep_index in range(ITERS):
         full_rows = lax.all_gather(iterate, "tensor", axis=0, tiled=True)
         gram_rows = against(iterate, full_rows)
-        full_gram = lax.all_gather(gram_rows, "tensor", axis=0, tiled=True)
+        full_gram = jnp.concatenate(
+            lax.all_to_all(jnp.stack([gram_rows] * lax.axis_size("tensor")), "tensor", 0, 0), axis=0
+        )
         square_rows = product(gram_rows, full_gram)
         polynomial = second_coef * gram_rows + third_coef * square_rows
         iterate = first_coef * iterate + product(polynomial, full_rows)

time: 522 us -> 510 us (0.977)
  blocking collectives: 125 us -> 278 us
  waiting for transfers between devices: 303 us -> 151 us
  matrix products: 55 us -> 42.4 us
    all_gather x3 -> x0, waiting for transfers between devices: 153 us -> none  [per_device(): full_gram = lax.all_gather(gram_rows, 'tensor', axis=0, tiled=True)]
    all_to_all x0 -> x3, blocking collectives: none -> 153 us  [per_device(): lax.all_to_all(jnp.stack([gram_rows] * lax.axis_size('tensor')), 'tensor'...]
    dot_general x6, matrix products: 33.2 us -> 24.6 us  [product(): jnp.einsum('ij,jl->il', left, right, precision=lax.Precision.HIGHEST, pre...]
  transfers between devices with their start and end apart: 6 -> 3, of which waited for: 6 -> 3; matrix products, arithmetic and copies ran while one was open for 0% -> 0% of each run, Pallas kernels for 0% -> 0%
where the time goes in v1:
time: 510 us; the launch traced here: 505 us
  blocking collectives  278 us (55%)
  waiting for transfers between devices  151 us (30%)
  matrix products  42.4 us (8%)
  between operations  14.9 us (3%)
  local copies, waits for them, and re-layouts  11.6 us (2%)
  other arithmetic  7.21 us (1%)
    all_to_all x3, blocking collectives, per_device(): lax.all_to_all(jnp.stack([gram_rows] * lax.axis_size('tensor')), 'tensor'...  153 us
    all_gather x3, waiting for transfers between devices, per_device(): full_rows = lax.all_gather(iterate, 'tensor', axis=0, tiled=True)  151 us
    all_to_all x1, blocking collectives, per_device(): lax.all_to_all(direction, 'shard', split_axis=0, concat_axis=0, tiled=True)  41.5 us
    all_to_all x1, blocking collectives, per_device(): lax.all_to_all(result, 'shard', split_axis=0, concat_axis=0, tiled=True)  40.3 us
    dot_general x6, matrix products, product(): jnp.einsum('ij,jl->il', left, right, precision=lax.Precision.HIGHEST, pre...  24.6 us
    all_to_all x1, blocking collectives, per_device(): lax.all_to_all(by_owner, 'tensor', split_axis=1, concat_axis=2, tiled=True)  18.7 us
    dot_general x3, matrix products, against(): jnp.einsum('ij,lj->il', left, right, precision=lax.Precision.HIGHEST, pre...  17.8 us
    all_to_all x1, blocking collectives, per_device(): lax.all_to_all(lax.all_to_all(result, 'shard', split_axis=0, concat_axis=...  17.4 us
  transfers between devices with their start and end apart: 3, of which 3 were waited for; matrix products, arithmetic and copies ran while one was open for 0% of the time, Pallas kernels for 0%

profile of v1, /device:TPU:1, one launch (start us, length us, event | category | flops | bytes accessed | tf_op | source)
XLA Modules:
  0.0 505.4 jit_solution(17944522268057107197)
XLA Ops:
  7.2 0.0 all-gather.4.cloned.1.call-start
  7.2 2.6 convert_add_fusion
  9.8 41.5 %all_to_all.52 = f32[64,16,256]{2,1,0:T(8,128)S(1)} all-to-all(f32[64,16,256]{2,1,0:T(8,128)S(1)} %get-tuple-element.4), channel_id=1, replica_groups=mesh['shard'=64,'tensor'=4] {'shard'}, dimensions={0} | all-to-all | bytes 2097152 | tf_op jit(solution)/shard_map/all_to_all | solution.py:40
  51.2 0.6 copy.12
  51.8 18.7 %all_to_all.53 = f32[64,16,256]{2,0,1:T(8,128)S(1)} all-to-all(f32[64,16,256]{2,0,1:T(8,128)S(1)} %copy.12), channel_id=1, replica_groups=mesh['shard'=64,'tensor'=4] {'tensor'}, dimensions={1} | all-to-all | bytes 2097152 | tf_op jit(solution)/shard_map/all_to_all | solution.py:41
  70.5 0.9 multiply_reduce_fusion
  71.4 7.6 %psum.7 = f32[]{:T(128)} all-reduce(f32[]{:T(128)} %multiply_reduce_fusion), channel_id=1, replica_groups=mesh['shard'=64,'tensor'=4] {'tensor'}, use_global_device_ids=true, to_apply=%region_1.0 | all-reduce | flops 1 | bytes 8 | tf_op jit(solution)/shard_map/psum | solution.py:46
  79.6 0.1 broadcast_divide_fusion
  79.7 0.7 copy.13
  80.4 1.2 copy.16
  81.6 0.0 all-gather.4.cloned.1.call-update
  81.6 0.0 all-gather.6.cloned.1.call-start
  81.6 47.9 %all-gather.4.cloned.1.call-done = f32[1024,1024]{1,0:T(8,128)} async-done(((f32[256,1024]{1,0:T(8,128)}), f32[1024,1024]{1,0:T(8,128)}) %all-gather.4.cloned.1.call-update) | async-done | bytes 4194320 | tf_op jit(solution)/shard_map/all_gather | solution.py:49
  129.6 5.9 %fusion.4 = f32[256,1024]{1,0:T(8,128)S(1)} fusion(f32[256,1024]{1,0:T(8,128)} %bitcast.35, f32[1024,1024]{1,0:T(8,128)} %all-gather.4.cloned.1.call-done), kind=kOutput, calls=%fused_computation.14 | convolution fusion | flops 3221225472 | bytes 6291456 | tf_op jit(solution)/shard_map/ij,lj->il/dot_general | solution.py:27
  135.5 0.5 stack.6
  136.1 50.9 %all_to_all.54 = f32[4,256,1024]{2,1,0:T(8,128)S(1)} all-to-all(f32[4,256,1024]{2,1,0:T(8,128)S(1)} %stack.6), channel_id=1, replica_groups=mesh['shard'=64,'tensor'=4] {'tensor'}, dimensions={0} | all-to-all | bytes 8388608 | tf_op jit(solution)/shard_map/all_to_all | solution.py:52
  187.0 0.0 copy-start
  187.0 0.0 copy-start.5
  187.0 3.8 fusion.3
  190.8 0.0 copy-done
  190.8 0.0 copy-done.5
  190.8 4.7 convolution_add_fusion.2
  195.5 0.0 all-gather.6.cloned.1.call-update
  195.5 0.0 all-gather.8.cloned.1.call-start
  195.6 51.5 %all-gather.6.cloned.1.call-done = f32[1024,1024]{1,0:T(8,128)} async-done(((f32[256,1024]{1,0:T(8,128)}), f32[1024,1024]{1,0:T(8,128)}) %all-gather.6.cloned.1.call-update) | async-done | bytes 4194320 | tf_op jit(solution)/shard_map/all_gather | solution.py:49
  247.0 5.9 %fusion.5 = f32[256,1024]{1,0:T(8,128)S(1)} fusion(f32[256,1024]{1,0:T(8,128)} %convolution_add_fusion.2, f32[1024,1024]{1,0:T(8,128)} %all-gather.6.cloned.1.call-done), kind=kOutput, calls=%fused_computation.15 | convolution fusion | flops 3221225472 | bytes 6291456 | tf_op jit(solution)/shard_map/ij,lj->il/dot_general | solution.py:27
  253.0 0.5 stack.7
  253.5 51.1 %all_to_all.55 = f32[4,256,1024]{2,1,0:T(8,128)S(1)} all-to-all(f32[4,256,1024]{2,1,0:T(8,128)S(1)} %stack.7), channel_id=1, replica_groups=mesh['shard'=64,'tensor'=4] {'tensor'}, dimensions={0} | all-to-all | bytes 8388608 | tf_op jit(solution)/shard_map/all_to_all | solution.py:52
  304.7 0.0 copy-start.1
  304.7 0.0 copy-start.3
  304.7 3.8 fusion.2
  308.5 0.0 copy-done.1
  308.5 0.0 copy-done.3
  308.5 4.7 convolution_add_fusion.1
  313.2 0.0 all-gather.8.cloned.1.call-update
  313.2 51.5 %all-gather.8.cloned.1.call-done = f32[1024,1024]{1,0:T(8,128)} async-done(((f32[256,1024]{1,0:T(8,128)}), f32[1024,1024]{1,0:T(8,128)}) %all-gather.8.cloned.1.call-update) | async-done | bytes 4194320 | tf_op jit(solution)/shard_map/all_gather | solution.py:49
  364.8 5.9 %fusion.6 = f32[256,1024]{1,0:T(8,128)S(1)} fusion(f32[256,1024]{1,0:T(8,128)} %convolution_add_fusion.1, f32[1024,1024]{1,0:T(8,128)} %all-gather.8.cloned.1.call-done), kind=kOutput, calls=%fused_computation.16 | convolution fusion | flops 3221225472 | bytes 6291456 | tf_op jit(solution)/shard_map/ij,lj->il/dot_general | solution.py:27
  370.7 0.5 stack.8
  371.2 50.8 %all_to_all.56 = f32[4,256,1024]{2,1,0:T(8,128)S(1)} all-to-all(f32[4,256,1024]{2,1,0:T(8,128)S(1)} %stack.8), channel_id=1, replica_groups=mesh['shard'=64,'tensor'=4] {'tensor'}, dimensions={0} | all-to-all | bytes 8388608 | tf_op jit(solution)/shard_map/all_to_all | solution.py:52
  422.0 0.0 copy-start.2
  422.0 0.0 copy-start.4
  422.0 3.8 fusion.1
  425.8 0.0 copy-done.2
  425.8 0.0 copy-done.4
  425.9 3.8 fusion
  429.6 0.3 reshape.32
  430.0 40.3 %all_to_all.57 = f32[64,4,1024]{2,1,0:T(4,128)S(1)} all-to-all(f32[64,4,1024]{2,1,0:T(4,128)S(1)} %reshape.32), channel_id=1, replica_groups=mesh['shard'=64,'tensor'=4] {'shard'}, dimensions={0} | all-to-all | bytes 2097152 | tf_op jit(solution)/shard_map/all_to_all | solution.py:59
  470.3 0.9 copy.14
  471.2 2.0 reshape.33
  473.2 17.4 %all_to_all.58 = f32[4,1,65536]{2,1,0:T(1,128)S(1)} all-to-all(f32[4,1,65536]{2,1,0:T(1,128)S(1)} %reshape.33), channel_id=1, replica_groups=mesh['shard'=64,'tensor'=4] {'tensor'}, dimensions={0} | all-to-all | bytes 2097152 | tf_op jit(solution)/shard_map/all_to_all | solution.py:58
  490.7 0.5 broadcast.40
  491.2 3.7 reduce.3
  494.9 1.4 reshape.34
  496.3 1.0 copy.15
  497.4 1.3 all_to_all.44
Async XLA Ops:
  7.2 122.4 %all-gather.4.cloned.1.call-start = ((), (), s32[]{:S(2)}) async-start(), calls=%async_computation.7 | async-start | bytes 5242880 | tf_op jit(solution)/shard_map/all_gather | solution.py:49
  81.6 165.4 %all-gather.6.cloned.1.call-start = ((), (), s32[]{:S(2)}) async-start(), calls=%async_computation.8 | async-start | bytes 5242880 | tf_op jit(solution)/shard_map/all_gather | solution.py:49
  187.0 3.8 copy-start
  187.0 3.8 copy-start.5
  195.5 169.2 %all-gather.8.cloned.1.call-start = ((), (), s32[]{:S(2)}) async-start(), calls=%async_computation.9 | async-start | bytes 5242880 | tf_op jit(solution)/shard_map/all_gather | solution.py:49
  304.7 3.8 copy-start.1
  304.7 3.8 copy-start.3
  422.0 3.8 copy-start.2
  422.0 3.8 copy-start.4
Sparse Core Ops, SparseCore 0:
  81.7 47.8 all-gather.3
  195.7 51.3 all-gather.5
  313.4 51.3 all-gather.7
